TPU v7x, 32 devices: a whole 2x2x4 slice. The times are simulated.
32 devices in a mesh: dp: 8 (over z, x), tp: 4 (over y, core).
Axes of the slice: x: 2, y: 2, z: 4, core: 2. Of those that a mesh axis runs over, the one named last changes fastest.
Arguments:
- activations: bfloat16 [2048, 4096], P('dp'), may hold values from -6 to 6
- out_grads: bfloat16 [2048, 4096], P('dp', 'tp'), may hold values from -6 to 6
- residual: bfloat16 [32768, 4096], P('dp', 'tp'), may hold values from -24 to 24
- right_prev: bfloat16 [4096, 32], P('tp'), may hold values from -6 to 6
Outputs:
- update: bfloat16 [4096, 4096], P(None, 'tp')
- left_basis: float32 [4096, 32], replicated
- right_factor: float32 [4096, 32], P('tp')
All inputs are finite; a program needn't handle non-finite values.
Results may differ from a plain program's by a relative error of at most 0.0061.
Values sent between devices are 32-bit elements; how exact they have to be, the bound alone decides.
A program may use at most 64 MiB of HBM per device.

v0:
```python
import jax
import jax.numpy as jnp
from jax import lax
from jax.sharding import PartitionSpec as P


def shards(activations, out_grads, residual, right_prev):
    product = lax.dot_general(
        activations, out_grads, (((0,), (0,)), ((), ())), preferred_element_type=jnp.float32
    )
    merged = (product + residual.astype(jnp.float32)).astype(jnp.bfloat16)
    shard_sum = lax.psum_scatter(
        jnp.dot(merged, right_prev, preferred_element_type=jnp.float32),
        "tp",
        scatter_dimension=0,
        tiled=True,
    )
    block_sum = lax.psum(shard_sum, "dp")
    block_gram = jnp.dot(block_sum.T, block_sum, precision=lax.Precision.HIGHEST)
    gram_matrix = lax.psum(block_gram, "tp")
    lower_factor = jnp.linalg.cholesky(gram_matrix)
    basis_block = lax.linalg.triangular_solve(
        lower_factor, block_sum, left_side=False, lower=True, transpose_a=True
    )
    left_basis = lax.all_gather(basis_block, "tp", axis=0, tiled=True)
    left_half = left_basis.astype(jnp.bfloat16)
    coeff_terms = lax.dot_general(
        merged, left_half, (((0,), (0,)), ((), ())), preferred_element_type=jnp.float32
    )
    right_factor = lax.psum(coeff_terms, "dp") / lax.axis_size("dp")
    update = jnp.dot(left_basis, right_factor.T, precision=lax.Precision.HIGHEST).astype(
        jnp.bfloat16
    )
    return (update, left_basis, right_factor)


def solution(mesh):
    in_specs = (P("dp", None), P("dp", "tp"), P("dp", "tp"), P("tp", None))
    out_specs = (P(None, "tp"), P(), P("tp", None))
    return jax.shard_map(shards, mesh=mesh, in_specs=in_specs, out_specs=out_specs, check_vma=False)
```

profile of v0, /device:TPU:0, one launch (start us, length us, event | category | flops | bytes accessed | tf_op | source)
XLA Modules:
  0.0 244.7 jit_solution(3257671253548092697)
XLA Ops:
  7.2 0.0 copy-start
  7.2 0.0 copy-start.3
  7.2 0.0 reduce-scatter.2.cloned.1.call-start
  7.2 1.5 copy-done
  8.8 6.0 %add_convert_fusion = bf16[4096,1024]{1,0:T(8,128)(2,1)S(1)} fusion(bf16[4096,1024]{1,0:T(8,128)(2,1)} %param.6, bf16[256,4096]{1,0:T(8,128)(2,1)S(1)} %copy-done, bf16[256,1024]{1,0:T(8,128)(2,1)} %param.5), kind=kOutput, calls=%fused_computation | convolution fusion | flops 2160066560 | bytes 19398656 | tf_op jit(solution)/shard_map/dot_general | solution.py:8
  14.7 0.0 copy-start.1
  14.7 3.4 %copy-done.1 = bf16[4096,1024]{1,0:T(8,128)(2,1)} copy-done((bf16[4096,1024]{1,0:T(8,128)(2,1)}, bf16[4096,1024]{1,0:T(8,128)(2,1)S(1)}, u32[]{:S(2)}) %copy-start.1) | copy-done | bytes 8388632
  18.1 0.0 copy-done.3
  18.1 3.4 %fusion.6 = f32[4096,32]{0,1:T(8,128)} fusion(bf16[4096,1024]{1,0:T(8,128)(2,1)S(1)} %add_convert_fusion, bf16[1024,32]{0,1:T(8,128)(2,1)S(1)} %copy-done.3), kind=kOutput, calls=%fused_computation.15 | convolution fusion | flops 268435456 | bytes 8978432 | tf_op jit(solution)/shard_map/dot_general | solution.py:13
  21.5 0.0 reduce-scatter.2.cloned.1.call-update
  21.5 0.0 all-reduce.3.cloned.1.call-start
  21.6 24.5 %reduce-scatter.2.cloned.1.call-done = f32[1024,32]{0,1:T(8,128)} async-done(((f32[4096,32]{0,1:T(8,128)}), f32[1024,32]{0,1:T(8,128)}) %reduce-scatter.2.cloned.1.call-update) | async-done | bytes 131088 | tf_op jit(solution)/shard_map/reduce_scatter | solution.py:12
  46.0 0.0 all-reduce.3.cloned.1.call-update
  46.1 0.0 all-reduce.5.cloned.1.call-start
  46.1 73.8 %all-reduce.3.cloned.1.call-done = f32[1024,32]{0,1:T(8,128)} async-done(((f32[1024,32]{0,1:T(8,128)}), f32[1024,32]{0,1:T(8,128)}) %all-reduce.3.cloned.1.call-update) | async-done | bytes 131088 | tf_op jit(solution)/shard_map/psum | solution.py:18
  119.9 1.2 fusion.7
  121.1 10.1 %psum.22 = f32[32,32]{0,1:T(8,128)S(1)} all-reduce(f32[32,32]{0,1:T(8,128)S(1)} %fusion.7), channel_id=1, replica_groups=mesh['dp'=8,'tp'=4] {'tp'}, use_global_device_ids=true, to_apply=%region_2.0 | all-reduce | flops 1024 | bytes 8192 | tf_op jit(solution)/shard_map/psum | solution.py:20
  131.3 0.1 copy.8
  131.3 2.9 %cholesky.16 = f32[32,32]{1,0:T(8,128)S(1)} custom-call(f32[32,32]{1,0:T(8,128)S(1)} %fusion.5), custom_call_target="Cholesky" | custom-call | tf_op jit(solution)/shard_map/jit(cholesky)/cholesky | solution.py:21
  134.3 0.6 compare_reduce_fusion
  134.9 0.7 fusion.2
  135.6 2.4 custom-call.6
  138.0 1.2 fusion.3
  139.3 7.3 %all_gather.3 = f32[4096,32]{0,1:T(8,128)S(1)} all-gather(f32[1024,32]{0,1:T(8,128)S(1)} %fusion.3), channel_id=1, replica_groups=mesh['dp'=8,'tp'=4] {'tp'}, dimensions={0}, use_global_device_ids=true | all-gather | bytes 655360 | tf_op jit(solution)/shard_map/all_gather | solution.py:25
  146.6 5.6 %fusion = f32[1024,32]{0,1:T(8,128)} fusion(bf16[4096,1024]{1,0:T(8,128)(2,1)} %copy-done.1, f32[4096,32]{0,1:T(8,128)S(1)} %all_gather.3), kind=kOutput, calls=%fused_computation.2 | convolution fusion | flops 268566528 | bytes 9043968 | tf_op jit(solution)/shard_map/dot_general | solution.py:27
  152.1 0.0 all-reduce.5.cloned.1.call-update
  152.2 69.1 %all-reduce.5.cloned.1.call-done = f32[1024,32]{0,1:T(8,128)} async-done(((f32[1024,32]{0,1:T(8,128)}), f32[1024,32]{0,1:T(8,128)}) %all-reduce.5.cloned.1.call-update) | async-done | bytes 131088 | tf_op jit(solution)/shard_map/psum | solution.py:30
  221.2 0.9 broadcast_multiply_fusion
  222.1 0.0 copy-start.2
  222.1 15.3 %convolution_convert_fusion = bf16[4096,1024]{1,0:T(8,128)(2,1)} fusion(f32[4096,32]{0,1:T(8,128)S(1)} %all_gather.3, f32[1024,32]{0,1:T(8,128)S(1)} %broadcast_multiply_fusion), kind=kOutput, calls=%fused_computation.1 | convolution fusion | flops 1614807040 | bytes 9043968 | tf_op jit(solution)/shard_map/dot_general | solution.py:31
  237.4 0.8 copy.13
  238.2 0.0 copy-done.2
  (2 shorter events, 0.0 us)
Async XLA Ops:
  7.2 1.6 copy-start
  7.2 10.9 %copy-start.3 = (bf16[1024,32]{0,1:T(8,128)(2,1)S(1)}, bf16[1024,32]{0,1:T(8,128)(2,1)}, u32[]{:S(2)}) copy-start(bf16[1024,32]{0,1:T(8,128)(2,1)} %param.7) | copy-start | bytes 196612
  7.2 38.8 %reduce-scatter.2.cloned.1.call-start = ((), (), s32[]{:S(2)}) async-start(), calls=%async_computation.1 | async-start | bytes 655360 | tf_op jit(solution)/shard_map/reduce_scatter | solution.py:12
  14.7 3.4 %copy-start.1 = (bf16[4096,1024]{1,0:T(8,128)(2,1)}, bf16[4096,1024]{1,0:T(8,128)(2,1)S(1)}, u32[]{:S(2)}) copy-start(bf16[4096,1024]{1,0:T(8,128)(2,1)S(1)} %add_convert_fusion) | copy-start | bytes 25165828
  21.5 98.4 %all-reduce.3.cloned.1.call-start = ((), (), s32[]{:S(2)}) async-start(), calls=%async_computation.2 | async-start | bytes 262144 | tf_op jit(solution)/shard_map/psum | solution.py:18
  46.1 175.2 %all-reduce.5.cloned.1.call-start = ((), (), s32[]{:S(2)}) async-start(), calls=%async_computation.3 | async-start | bytes 262144 | tf_op jit(solution)/shard_map/psum | solution.py:30
  222.1 16.1 %copy-start.2 = (f32[1024,32]{0,1:T(8,128)}, f32[1024,32]{0,1:T(8,128)S(1)}, u32[]{:S(2)}) copy-start(f32[1024,32]{0,1:T(8,128)S(1)} %broadcast_multiply_fusion) | copy-start | bytes 393220
Sparse Core Ops, SparseCore 0:
  21.6 24.3 reduce-scatter.1
  49.4 70.4 all-reduce.2
  152.3 68.8 all-reduce.4
where the time goes:
time: 245 us
  waiting for transfers between devices  167 us (68%)
  matrix products  32.6 us (13%)
  blocking collectives  17.4 us (7%)
  between operations  13.8 us (6%)
  other arithmetic  7.6 us (3%)
  local copies, waits for them, and re-layouts  5.8 us (2%)
    psum x1, waiting for transfers between devices, shards(): block_sum = lax.psum(shard_sum, 'dp')  73.8 us
    psum x1, waiting for transfers between devices, shards(): right_factor = lax.psum(coeff_terms, 'dp') / lax.axis_size('dp')  69.1 us
    reduce_scatter x1, waiting for transfers between devices, shards(): lax.psum_scatter(jnp.dot(merged, right_prev, preferred_element_type=jnp.f...  24.5 us
    dot_general x1, matrix products, shards(): jnp.dot(left_basis, right_factor.T, precision=lax.Precision.HIGHEST)  15.3 us
    psum x1, blocking collectives, shards(): gram_matrix = lax.psum(block_gram, 'tp')  10.1 us
    all_gather x1, blocking collectives, shards(): left_basis = lax.all_gather(basis_block, 'tp', axis=0, tiled=True)  7.28 us
    dot_general x1, matrix products, shards(): lax.dot_general(activations, out_grads, (((0,), (0,)), ((), ())), preferr...  5.95 us
    unnamed x9, local copies, waits for them, and re-layouts  5.73 us
  transfers between devices with their start and end apart: 3, of which 3 were waited for; matrix products, arithmetic and copies ran while one was open for 0% of the time, Pallas kernels for 0%

commit v1 on v0

--- a/solution.py
+++ b/solution.py
@@ -27,7 +27,7 @@
     coeff_terms = lax.dot_general(
         merged, left_half, (((0,), (0,)), ((), ())), preferred_element_type=jnp.float32
     )
-    right_factor = lax.psum(coeff_terms, "dp") / lax.axis_size("dp")
+    right_factor = jnp.sum(lax.all_gather(coeff_terms, "dp"), axis=0) / lax.axis_size("dp")
     update = jnp.dot(left_basis, right_factor.T, precision=lax.Precision.HIGHEST).astype(
         jnp.bfloat16
     )

time: 245 us -> 216 us (0.88)
  waiting for transfers between devices: 167 us -> 137 us
    psum x1 -> x0, waiting for transfers between devices: 69.1 us -> none  [shards(): right_factor = lax.psum(coeff_terms, 'dp') / lax.axis_size('dp')]
    all_gather x0 -> x1, waiting for transfers between devices: none -> 38.9 us  [shards(): lax.all_gather(coeff_terms, 'dp')]
    unnamed x9 -> x10, local copies, waits for them, and re-layouts: 5.73 us -> 7.56 us
where the time goes in v1:
time: 216 us
  waiting for transfers between devices  137 us (63%)
  matrix products  32.6 us (15%)
  blocking collectives  17.4 us (8%)
  between operations  13.8 us (6%)
  local copies, waits for them, and re-layouts  7.64 us (4%)
  other arithmetic  6.96 us (3%)
    psum x1, waiting for transfers between devices, shards(): block_sum = lax.psum(shard_sum, 'dp')  73.8 us
    all_gather x1, waiting for transfers between devices, shards(): lax.all_gather(coeff_terms, 'dp')  38.9 us
    reduce_scatter x1, waiting for transfers between devices, shards(): lax.psum_scatter(jnp.dot(merged, right_prev, preferred_element_type=jnp.f...  24.5 us
    dot_general x1, matrix products, shards(): jnp.dot(left_basis, right_factor.T, precision=lax.Precision.HIGHEST)  15.3 us
    psum x1, blocking collectives, shards(): gram_matrix = lax.psum(block_gram, 'tp')  10.1 us
    unnamed x10, local copies, waits for them, and re-layouts  7.56 us
    all_gather x1, blocking collectives, shards(): left_basis = lax.all_gather(basis_block, 'tp', axis=0, tiled=True)  7.28 us
    dot_general x1, matrix products, shards(): lax.dot_general(activations, out_grads, (((0,), (0,)), ((), ())), preferr...  5.95 us
  transfers between devices with their start and end apart: 3, of which 3 were waited for; matrix products, arithmetic and copies ran while one was open for 0% of the time, Pallas kernels for 0%

profile of v1, /device:TPU:0, one launch (start us, length us, event | category | flops | bytes accessed | tf_op | source)
XLA Modules:
  0.0 215.7 jit_solution(14165289614508684784)
XLA Ops:
  7.2 0.0 copy-start
  7.2 0.0 copy-start.3
  7.2 0.0 reduce-scatter.2.cloned.1.call-start
  7.2 1.5 copy-done
  8.8 6.0 %add_convert_fusion = bf16[4096,1024]{1,0:T(8,128)(2,1)S(1)} fusion(bf16[4096,1024]{1,0:T(8,128)(2,1)} %param.6, bf16[256,4096]{1,0:T(8,128)(2,1)S(1)} %copy-done, bf16[256,1024]{1,0:T(8,128)(2,1)} %param.5), kind=kOutput, calls=%fused_computation | convolution fusion | flops 2160066560 | bytes 19398656 | tf_op jit(solution)/shard_map/dot_general | solution.py:8
  14.7 0.0 copy-start.1
  14.7 3.4 %copy-done.1 = bf16[4096,1024]{1,0:T(8,128)(2,1)} copy-done((bf16[4096,1024]{1,0:T(8,128)(2,1)}, bf16[4096,1024]{1,0:T(8,128)(2,1)S(1)}, u32[]{:S(2)}) %copy-start.1) | copy-done | bytes 8388632
  18.1 0.0 copy-done.3
  18.1 3.4 %fusion.6 = f32[4096,32]{0,1:T(8,128)} fusion(bf16[4096,1024]{1,0:T(8,128)(2,1)S(1)} %add_convert_fusion, bf16[1024,32]{0,1:T(8,128)(2,1)S(1)} %copy-done.3), kind=kOutput, calls=%fused_computation.16 | convolution fusion | flops 268435456 | bytes 8978432 | tf_op jit(solution)/shard_map/dot_general | solution.py:13
  21.5 0.0 reduce-scatter.2.cloned.1.call-update
  21.5 0.0 all-reduce.2.cloned.1.call-start
  21.6 24.5 %reduce-scatter.2.cloned.1.call-done = f32[1024,32]{0,1:T(8,128)} async-done(((f32[4096,32]{0,1:T(8,128)}), f32[1024,32]{0,1:T(8,128)}) %reduce-scatter.2.cloned.1.call-update) | async-done | bytes 131088 | tf_op jit(solution)/shard_map/reduce_scatter | solution.py:12
  46.0 0.0 all-reduce.2.cloned.1.call-update
  46.1 0.0 all-gather.3.cloned.1.call-start
  46.1 73.8 %all-reduce.2.cloned.1.call-done = f32[1024,32]{0,1:T(8,128)} async-done(((f32[1024,32]{0,1:T(8,128)}), f32[1024,32]{0,1:T(8,128)}) %all-reduce.2.cloned.1.call-update) | async-done | bytes 131088 | tf_op jit(solution)/shard_map/psum | solution.py:18
  119.9 1.2 fusion.7
  121.1 10.1 %psum.15 = f32[32,32]{0,1:T(8,128)S(1)} all-reduce(f32[32,32]{0,1:T(8,128)S(1)} %fusion.7), channel_id=1, replica_groups=mesh['dp'=8,'tp'=4] {'tp'}, use_global_device_ids=true, to_apply=%region_2.0 | all-reduce | flops 1024 | bytes 8192 | tf_op jit(solution)/shard_map/psum | solution.py:20
  131.3 0.1 copy.8
  131.3 2.9 %cholesky.16 = f32[32,32]{1,0:T(8,128)S(1)} custom-call(f32[32,32]{1,0:T(8,128)S(1)} %fusion.5), custom_call_target="Cholesky" | custom-call | tf_op jit(solution)/shard_map/jit(cholesky)/cholesky | solution.py:21
  134.3 0.6 compare_reduce_fusion
  134.9 0.7 fusion.2
  135.6 2.4 %custom-call.6 = f32[1,32,32]{1,2,0:T(8,128)S(1)} custom-call(f32[1,32,32]{2,1,0:T(8,128)S(1)} %fusion.2), custom_call_target="InvertDiagBlocksLowerTriangular" | custom-call | tf_op jit(solution)/shard_map/triangular_solve | solution.py:22
  138.0 1.2 fusion.3
  139.3 7.3 %all_gather.9 = f32[4096,32]{0,1:T(8,128)S(1)} all-gather(f32[1024,32]{0,1:T(8,128)S(1)} %fusion.3), channel_id=1, replica_groups=mesh['dp'=8,'tp'=4] {'tp'}, dimensions={0}, use_global_device_ids=true | all-gather | bytes 655360 | tf_op jit(solution)/shard_map/all_gather | solution.py:25
  146.6 5.6 %fusion = f32[1024,32]{0,1:T(8,128)} fusion(bf16[4096,1024]{1,0:T(8,128)(2,1)} %copy-done.1, f32[4096,32]{0,1:T(8,128)S(1)} %all_gather.9), kind=kOutput, calls=%fused_computation.3 | convolution fusion | flops 268566528 | bytes 9043968 | tf_op jit(solution)/shard_map/dot_general | solution.py:27
  152.1 0.0 all-gather.3.cloned.1.call-update
  152.2 38.9 %all-gather.3.cloned.1.call-done = f32[8192,32]{0,1:T(8,128)} async-done(((f32[1024,32]{0,1:T(8,128)}), f32[8192,32]{0,1:T(8,128)}) %all-gather.3.cloned.1.call-update) | async-done | bytes 1048592 | tf_op jit(solution)/shard_map/all_gather | solution.py:30
  191.0 1.8 copy.10
  192.9 0.3 bitcast_reduce_fusion
  193.1 0.0 copy-start.2
  193.2 15.3 %convolution_convert_fusion = bf16[4096,1024]{1,0:T(8,128)(2,1)} fusion(f32[4096,32]{0,1:T(8,128)S(1)} %all_gather.9, f32[1024,32]{0,1:T(8,128)S(1)} %broadcast_multiply_fusion), kind=kOutput, calls=%fused_computation.1 | convolution fusion | flops 1614807040 | bytes 9043968 | tf_op jit(solution)/shard_map/dot_general | solution.py:31
  208.4 0.8 copy.13
  209.2 0.0 copy-done.2
  (3 shorter events, 0.1 us)
Async XLA Ops:
  7.2 1.6 copy-start
  7.2 10.9 %copy-start.3 = (bf16[1024,32]{0,1:T(8,128)(2,1)S(1)}, bf16[1024,32]{0,1:T(8,128)(2,1)}, u32[]{:S(2)}) copy-start(bf16[1024,32]{0,1:T(8,128)(2,1)} %param.7) | copy-start | bytes 196612
  7.2 38.8 %reduce-scatter.2.cloned.1.call-start = ((), (), s32[]{:S(2)}) async-start(), calls=%async_computation.1 | async-start | bytes 655360 | tf_op jit(solution)/shard_map/reduce_scatter | solution.py:12
  14.7 3.4 %copy-start.1 = (bf16[4096,1024]{1,0:T(8,128)(2,1)}, bf16[4096,1024]{1,0:T(8,128)(2,1)S(1)}, u32[]{:S(2)}) copy-start(bf16[4096,1024]{1,0:T(8,128)(2,1)S(1)} %add_convert_fusion) | copy-start | bytes 25165828
  21.5 98.4 %all-reduce.2.cloned.1.call-start = ((), (), s32[]{:S(2)}) async-start(), calls=%async_computation.2 | async-start | bytes 262144 | tf_op jit(solution)/shard_map/psum | solution.py:18
  46.1 145.0 %all-gather.3.cloned.1.call-start = ((), (), s32[]{:S(2)}) async-start(), calls=%async_computation.3 | async-start | bytes 1179648 | tf_op jit(solution)/shard_map/all_gather | solution.py:30
  193.1 16.1 %copy-start.2 = (f32[1024,32]{0,1:T(8,128)}, f32[1024,32]{0,1:T(8,128)S(1)}, u32[]{:S(2)}) copy-start(f32[1024,32]{0,1:T(8,128)S(1)} %broadcast_multiply_fusion) | copy-start | bytes 393220
Sparse Core Ops, SparseCore 0:
  21.6 24.3 reduce-scatter.1
  49.4 70.4 all-reduce.1
  152.3 38.6 all-gather.2
